TPU v7x, 32 devices: a whole 2x2x4 slice. The times are simulated.
32 devices in a mesh: pb: 8 (over y, x, core), row: 4 (over z).
Axes of the slice: x: 2, y: 2, z: 4, core: 2. Of those that a mesh axis runs over, the one named last changes fastest.
Arguments:
- screened: bfloat16 [16, 2, 1024, 1024], P('pb', None, 'row'), may hold values from -1.0546875 to 1.0546875
- response: bfloat16 [16, 2, 1024, 1024], P(None, None, 'pb', 'row'), may hold values from -0.1875 to 0.1875
- q_owner: int32 [16], replicated, may hold values from 0 to 15, each once
- g_index: int32 [16, 1024], P('pb'), may hold values from 0 to 1023, each once within a row
Outputs:
- tangent: float32 [16, 2, 1024, 1024], P(None, None, ('row', 'pb'))
Inputs may be any that keep to these rules, and one draw needn't show every extreme that they name: `q_owner`: each owner slot appears once. `g_index`: each row is a permutation of the 1024 plane waves.
All inputs are finite; a program needn't handle non-finite values.
Results may differ from a plain program's by a relative error of at most 0.0029.
Values may be sent and summed in bfloat16 or wider, within the bound.
A program may use at most 64 MiB of HBM per device.

v0:
```python
import jax
import jax.numpy as jnp
from jax import lax
from jax.sharding import PartitionSpec as P


def complex_product(left, right):

    def product(first, second):
        return jnp.einsum("qik,qkj->qij", first, second, preferred_element_type=jnp.float32)

    real_part = product(left[:, 0], right[:, 0]) - product(left[:, 1], right[:, 1])
    imag_part = product(left[:, 0], right[:, 1]) + product(left[:, 1], right[:, 0])
    return jnp.stack((real_part, imag_part), axis=1)


def body(screened, response, q_owner, g_index):
    slot_count = q_owner.shape[0]
    inverse = (
        jnp.zeros((slot_count,), jnp.int32).at[q_owner].set(jnp.arange(slot_count, dtype=jnp.int32))
    )
    ordered = jnp.take(response, inverse, axis=0)
    at_owner = lax.all_to_all(ordered, "pb", split_axis=0, concat_axis=2, tiled=True)
    permuted = jax.vmap(lambda block, table: block[:, table, :])(at_owner, g_index)
    whole = lax.all_gather(screened, "row", axis=2, tiled=True)
    column_half = complex_product(whole, permuted).astype(jnp.bfloat16)
    halfway = lax.all_to_all(column_half, "row", split_axis=2, concat_axis=3, tiled=True)
    result = complex_product(halfway, whole)
    returned = lax.all_to_all(result, "pb", split_axis=2, concat_axis=0, tiled=True)
    return jnp.take(returned, q_owner, axis=0)


def solution(mesh):
    return jax.shard_map(
        body,
        mesh=mesh,
        in_specs=(P("pb", None, "row", None), P(None, None, "pb", "row"), P(), P("pb", None)),
        out_specs=P(None, None, ("row", "pb"), None),
        check_vma=False,
    )
```

profile of v0, /device:TPU:0, one launch (start us, length us, event | category | flops | bytes accessed | tf_op | source)
XLA Modules:
  0.0 326.9 jit_solution(15050981554449693041)
XLA Ops:
  6.5 3.2 copy.32
  9.8 0.6 copy-done.4
  10.4 0.6 scatter_custom_fusion
  11.1 2.0 gather_fusion
  13.1 3.2 broadcast_select_fusion.1
  16.3 5.3 %all-to-all-start = ((bf16[16,2,128,256]{3,2,1,0:T(8,128)(2,1)}), bf16[16,2,128,256]{3,2,1,0:T(8,128)(2,1)}, u32[]{:S(2)}, u32[]{:S(2)}) async-start(bf16[16,2,128,256]{3,2,1,0:T(8,128)(2,1)} %broadcast_select_fusion.1), calls=%async_computation | async-start | bytes 4194304 | tf_op jit(solution)/shard_map/all_to_all | solution.py:23
  21.7 26.7 %all-to-all-done = bf16[16,2,128,256]{3,2,1,0:T(8,128)(2,1)} async-done(((bf16[16,2,128,256]{3,2,1,0:T(8,128)(2,1)}), bf16[16,2,128,256]{3,2,1,0:T(8,128)(2,1)}, u32[]{:S(2)}, u32[]{:S(2)}) %all-to-all-start) | async-done | bytes 2097184 | tf_op jit(solution)/shard_map/all_to_all | solution.py:23
  48.3 1.7 copy.28
  50.1 3.5 %copy.29 = bf16[2,2,1024,256]{3,1,2,0:T(2,128)(2,1)} copy(bf16[2,2,1024,256]{3,2,1,0:T(8,128)(2,1)S(1)} %bitcast.86) | data formatting | bytes 4194304 | tf_op jit(solution)/shard_map/all_to_all | solution.py:23
  53.6 20.5 %gather_fusion.2 = bf16[2048,2,256]{2,1,0:T(2,128)(2,1)} fusion(bf16[2,2,1024,256]{3,1,2,0:T(2,128)(2,1)} %copy.29, s32[2048]{0:T(1024)S(1)} %bitcast.80), kind=kCustom, calls=%fused_computation.2 | custom fusion | bytes 4210688 | tf_op jit(solution)/shard_map/vmap()/gather | solution.py:24
  74.1 4.7 %copy.31 = bf16[2,1024,2,256]{1,3,0,2:T(8,128)(2,1)S(1)} copy(bf16[2,1024,2,256]{3,2,1,0:T(2,128)(2,1)} %bitcast.85) | data formatting | bytes 4194304 | tf_op jit(solution)/shard_map/vmap()/gather | solution.py:24
  78.8 83.5 %all-gather.2.cloned.1.call-done = bf16[2,2,1024,1024]{3,2,0,1:T(8,128)(2,1)} async-done(((bf16[2,2,256,1024]{3,2,0,1:T(8,128)(2,1)}), bf16[2,2,1024,1024]{3,2,0,1:T(8,128)(2,1)}) %all-gather.2.cloned.1.call-update) | async-done | bytes 8388624 | tf_op jit(solution)/shard_map/all_gather | solution.py:25
  162.3 3.6 %fusion.3 = f32[2,256,1024]{2,1,0:T(8,128)S(1)} fusion(bf16[2,2,1024,1024]{3,2,0,1:T(8,128)(2,1)} %all-gather.2.cloned.1.call-done, bf16[2,2,1024,256]{2,3,0,1:T(8,128)(2,1)S(1)} %bitcast.89), kind=kOutput, calls=%fused_computation.10 | convolution fusion | flops 1073741824 | bytes 7340032 | tf_op jit(solution)/shard_map/qik,qkj->qij/dot_general | solution.py:10
  165.9 1.0 copy-done.2
  166.9 1.4 fusion.2
  168.3 1.4 fusion.8
  169.8 1.4 fusion.9
  171.4 4.0 %copy.33 = bf16[2,2,1024,256]{3,0,1,2:T(2,128)(2,1)} copy(bf16[2,2,1024,256]{2,3,0,1:T(8,128)(2,1)S(1)} %pad_maximum_fusion.1) | data formatting | bytes 4194304 | tf_op jit(solution)/shard_map/stack | solution.py:14
  175.4 52.2 %all_to_all.54 = bf16[2,2,1024,256]{3,0,1,2:T(2,128)(2,1)S(1)} all-to-all(bf16[2,2,1024,256]{3,0,1,2:T(2,128)(2,1)} %copy.33), channel_id=1, replica_groups=mesh['pb'=8,'row'=4] {'row'}, dimensions={2} | all-to-all | bytes 4194304 | tf_op jit(solution)/shard_map/all_to_all | solution.py:27
  227.6 2.9 copy.43
  230.6 3.2 all_to_all.46
  233.8 3.6 %fusion.1 = f32[2,256,1024]{2,1,0:T(8,128)S(1)} fusion(bf16[2,2,1024,1024]{3,2,0,1:T(8,128)(2,1)} %all-gather.2.cloned.1.call-done, bf16[2,2,256,1024]{3,2,0,1:T(8,128)(2,1)S(1)} %all_to_all.46), kind=kOutput, calls=%fused_computation.8 | convolution fusion | flops 1073741824 | bytes 7340032 | tf_op jit(solution)/shard_map/qik,qkj->qij/dot_general | solution.py:10
  237.4 3.6 %fusion = f32[2,256,1024]{2,1,0:T(8,128)S(1)} fusion(bf16[2,2,1024,1024]{3,2,0,1:T(8,128)(2,1)} %all-gather.2.cloned.1.call-done, bf16[2,2,256,1024]{3,2,0,1:T(8,128)(2,1)S(1)} %all_to_all.46), kind=kOutput, calls=%fused_computation.7 | convolution fusion | flops 1073741824 | bytes 7340032 | tf_op jit(solution)/shard_map/qik,qkj->qij/dot_general | solution.py:10
  241.1 1.3 subtract_bitcast_fusion
  242.4 1.3 add_bitcast_fusion
  244.0 5.2 %copy.35 = f32[2,2,256,1024]{3,0,1,2:T(2,128)} copy(f32[2,2,256,1024]{3,2,0,1:T(8,128)S(1)} %pad_maximum_fusion) | data formatting | bytes 8388608 | tf_op jit(solution)/shard_map/stack | solution.py:14
  249.3 4.8 %all-to-all-start.2 = ((f32[2,2,256,1024]{3,0,1,2:T(2,128)}), f32[2,2,256,1024]{3,0,1,2:T(2,128)}, u32[]{:S(2)}, u32[]{:S(2)}) async-start(f32[2,2,256,1024]{3,0,1,2:T(2,128)} %copy.35), calls=%async_computation.2 | async-start | bytes 8388608 | tf_op jit(solution)/shard_map/all_to_all | solution.py:29
  254.1 48.8 %all-to-all-done.2 = f32[2,2,256,1024]{3,0,1,2:T(2,128)} async-done(((f32[2,2,256,1024]{3,0,1,2:T(2,128)}), f32[2,2,256,1024]{3,0,1,2:T(2,128)}, u32[]{:S(2)}, u32[]{:S(2)}) %all-to-all-start.2) | async-done | bytes 4194336 | tf_op jit(solution)/shard_map/all_to_all | solution.py:29
  302.9 4.6 %copy.36 = f32[2,2,256,1024]{3,2,1,0:T(8,128)S(1)} copy(f32[2,2,256,1024]{3,0,1,2:T(2,128)} %all-to-all-done.2) | data formatting | bytes 8388608 | tf_op jit(solution)/shard_map/all_to_all | solution.py:29
  307.5 2.3 copy.37
  309.9 4.9 %gather_fusion.1 = f32[16,2,32,1024]{3,2,1,0:T(8,128)} fusion(f32[16,2,32,1024]{3,2,1,0:T(8,128)} %bitcast.81, s32[1024]{0:T(1024)S(1)} %pad_clamp_fusion), kind=kCustom, calls=%fused_computation.1 | custom fusion | bytes 8388672 | tf_op jit(solution)/shard_map/jit(_take)/gather | solution.py:30
  314.8 5.3 %broadcast_select_fusion = f32[16,2,32,1024]{3,2,1,0:T(8,128)} fusion(f32[16,2,32,1024]{3,2,1,0:T(8,128)} %gather_fusion.1, pred[16]{0:T(512)(128)(4,1)S(1)} %compare_and_fusion.1), kind=kLoop, calls=%fused_computation.17 | loop fusion | flops 1048576 | bytes 8388624 | tf_op jit(solution)/shard_map/jit(_take)/select_n | solution.py:30
  (26 shorter events, 0.6 us)
Async XLA Ops:
  6.5 4.6 %copy-start = (bf16[16,2,128,256]{3,2,1,0:T(8,128)(2,1)S(1)}, bf16[16,2,128,256]{3,2,1,0:T(8,128)(2,1)}, u32[]{:S(2)}) copy-start(bf16[16,2,128,256]{3,2,1,0:T(8,128)(2,1)} %param.5) | copy-start | bytes 6291460
  6.5 155.7 %all-gather.2.cloned.1.call-start = ((), (), s32[]{:S(2)}) async-start(), calls=%async_computation.3 | async-start | bytes 10485760 | tf_op jit(solution)/shard_map/all_gather | solution.py:25
  9.8 0.7 copy-start.4
  16.3 5.3 %copy-start.3 = (s32[2,1024]{1,0:T(2,128)S(1)}, s32[2,1024]{1,0:T(2,128)}, u32[]{:S(2)}) copy-start(s32[2,1024]{1,0:T(2,128)} %param.7) | copy-start | bytes 24580
  16.3 32.0 %all-to-all-start = ((bf16[16,2,128,256]{3,2,1,0:T(8,128)(2,1)}), bf16[16,2,128,256]{3,2,1,0:T(8,128)(2,1)}, u32[]{:S(2)}, u32[]{:S(2)}) async-start(bf16[16,2,128,256]{3,2,1,0:T(8,128)(2,1)} %broadcast_select_fusion.1), calls=%async_computation | async-start | bytes 4194304 | tf_op jit(solution)/shard_map/all_to_all | solution.py:23
  162.3 4.6 %copy-start.2 = (bf16[2,2,1024,1024]{3,2,0,1:T(8,128)(2,1)S(1)}, bf16[2,2,1024,1024]{3,2,0,1:T(8,128)(2,1)}, u32[]{:S(2)}) copy-start(bf16[2,2,1024,1024]{3,2,0,1:T(8,128)(2,1)} %all-gather.2.cloned.1.call-done) | copy-start | bytes 25165828
  233.8 7.2 %slice-start = ((s8[8388608]{0:T(1024)(128)(4,1)}), s8[4194304]{0:T(1024)(128)(4,1)S(1)}, s32[]{:S(2)}) async-start(s8[8388608]{0:T(1024)(128)(4,1)} %bitcast.83), calls=%async_computation.4 | async-start | bytes 8388608
  237.4 3.6 %slice-start.1 = ((s8[8388608]{0:T(1024)(128)(4,1)}), s8[4194304]{0:T(1024)(128)(4,1)S(1)}, s32[]{:S(2)}) async-start(s8[8388608]{0:T(1024)(128)(4,1)} %bitcast.83), calls=%async_computation.5 | async-start | bytes 8388608
  249.3 53.7 %all-to-all-start.2 = ((f32[2,2,256,1024]{3,0,1,2:T(2,128)}), f32[2,2,256,1024]{3,0,1,2:T(2,128)}, u32[]{:S(2)}, u32[]{:S(2)}) async-start(f32[2,2,256,1024]{3,0,1,2:T(2,128)} %copy.35), calls=%async_computation.2 | async-start | bytes 8388608 | tf_op jit(solution)/shard_map/all_to_all | solution.py:29
  314.8 5.3 %copy-start.1 = (bf16[16,2,128,256]{3,2,1,0:T(8,128)(2,1)S(1)}, bf16[16,2,128,256]{3,2,1,0:T(8,128)(2,1)}, u32[]{:S(2)}) copy-start(bf16[16,2,128,256]{3,2,1,0:T(8,128)(2,1)} %param.5) | copy-start | bytes 6291460
Sparse Core Ops, SparseCore 0:
  9.9 152.3 all-gather.1
where the time goes:
time: 328 us; the launch traced here: 327 us
  waiting for transfers between devices  159 us (48%)
  local copies, waits for them, and re-layouts  65.4 us (20%)
  blocking collectives  52.2 us (16%)
  matrix products  17.6 us (5%)
  between operations  13.6 us (4%)
  starting transfers between devices  10.1 us (3%)
  other arithmetic  9.02 us (3%)
    all_gather x1, waiting for transfers between devices, body(): whole = lax.all_gather(screened, 'row', axis=2, tiled=True)  83.5 us
    all_to_all x1, blocking collectives, body(): lax.all_to_all(column_half, 'row', split_axis=2, concat_axis=3, tiled=True)  52.2 us
    all_to_all x1, waiting for transfers between devices, body(): lax.all_to_all(result, 'pb', split_axis=2, concat_axis=0, tiled=True)  48.8 us
    all_to_all x1, waiting for transfers between devices, body(): lax.all_to_all(ordered, 'pb', split_axis=0, concat_axis=2, tiled=True)  26.7 us
    gather x2, local copies, waits for them, and re-layouts, body(): block[:, table, :]  25.2 us
    dot_general x8, matrix products, product(): jnp.einsum('qik,qkj->qij', first, second, preferred_element_type=jnp.floa...  17.6 us
    another operation x2, local copies, waits for them, and re-layouts, complex_product(): return jnp.stack((real_part, imag_part), axis=1)  9.3 us
    all_to_all x2, local copies, waits for them, and re-layouts, body(): lax.all_to_all(result, 'pb', split_axis=2, concat_axis=0, tiled=True)  6.94 us
  transfers between devices with their start and end apart: 3, of which 3 were waited for; matrix products, arithmetic and copies ran while one was open for 11% of the time, Pallas kernels for 0%

commit v1 on v0

--- a/solution.py
+++ b/solution.py
@@ -24,7 +24,9 @@
     permuted = jax.vmap(lambda block, table: block[:, table, :])(at_owner, g_index)
     whole = lax.all_gather(screened, "row", axis=2, tiled=True)
     column_half = complex_product(whole, permuted).astype(jnp.bfloat16)
-    halfway = lax.all_to_all(column_half, "row", split_axis=2, concat_axis=3, tiled=True)
+    moved = jnp.split(column_half, jax.lax.axis_size("row"), axis=2)
+    base_arr = jnp.stack(moved)
+    halfway = jnp.concatenate(jax.lax.all_to_all(base_arr, "row", 0, 0), axis=3)
     result = complex_product(halfway, whole)
     returned = lax.all_to_all(result, "pb", split_axis=2, concat_axis=0, tiled=True)
     return jnp.take(returned, q_owner, axis=0)

time: 328 us -> 312 us (0.951)
  local copies, waits for them, and re-layouts: 65.4 us -> 55.2 us
  matrix products: 17.6 us -> 13.2 us
    all_to_all x2 -> x0, local copies, waits for them, and re-layouts: 6.17 us -> none  [body(): lax.all_to_all(column_half, 'row', split_axis=2, concat_axis=3, tiled=True)]
    dot_general x8, matrix products: 17.6 us -> 13.2 us  [product(): jnp.einsum('qik,qkj->qij', first, second, preferred_element_type=jnp.floa...]
    another operation x2 -> x1, local copies, waits for them, and re-layouts: 9.3 us -> 5.25 us  [complex_product(): return jnp.stack((real_part, imag_part), axis=1)]
  transfers between devices with their start and end apart: 3 -> 3, of which waited for: 3 -> 3; matrix products, arithmetic and copies ran while one was open for 11% -> 12% of each run, Pallas kernels for 0% -> 0%
where the time goes in v1:
time: 312 us
  waiting for transfers between devices  159 us (51%)
  local copies, waits for them, and re-layouts  55.2 us (18%)
  blocking collectives  51.1 us (16%)
  between operations  13.6 us (4%)
  matrix products  13.2 us (4%)
  starting transfers between devices  10.1 us (3%)
  other arithmetic  9.29 us (3%)
    all_gather x1, waiting for transfers between devices, body(): whole = lax.all_gather(screened, 'row', axis=2, tiled=True)  83.6 us
    all_to_all x1, blocking collectives, body(): halfway = jnp.concatenate(jax.lax.all_to_all(base_arr, 'row', 0, 0), axis=3)  51.1 us
    all_to_all x1, waiting for transfers between devices, body(): lax.all_to_all(result, 'pb', split_axis=2, concat_axis=0, tiled=True)  48.8 us
    all_to_all x1, waiting for transfers between devices, body(): lax.all_to_all(ordered, 'pb', split_axis=0, concat_axis=2, tiled=True)  26.7 us
    gather x2, local copies, waits for them, and re-layouts, body(): block[:, table, :]  25.1 us
    dot_general x8, matrix products, product(): jnp.einsum('qik,qkj->qij', first, second, preferred_element_type=jnp.floa...  13.2 us
    all_to_all x2, local copies, waits for them, and re-layouts, body(): lax.all_to_all(result, 'pb', split_axis=2, concat_axis=0, tiled=True)  6.94 us
  transfers between devices with their start and end apart: 3, of which 3 were waited for; matrix products, arithmetic and copies ran while one was open for 12% of the time, Pallas kernels for 0%

profile of v1, /device:TPU:0, one launch (start us, length us, event | category | flops | bytes accessed | tf_op | source)
XLA Modules:
  0.0 311.5 jit_solution(4930561816397734482)
XLA Ops:
  6.5 3.2 %copy.36 = bf16[2,2,256,1024]{3,2,0,1:T(8,128)(2,1)} copy(bf16[2,2,256,1024]{3,2,1,0:T(8,128)(2,1)} %param.4) | data formatting | bytes 4194304 | tf_op args[0]
  9.8 0.6 copy-done.4
  10.4 0.6 scatter_custom_fusion
  11.1 2.0 gather_fusion
  13.1 3.2 %broadcast_select_fusion.1 = bf16[16,2,128,256]{3,2,1,0:T(8,128)(2,1)} fusion(bf16[16,2,128,256]{3,2,1,0:T(8,128)(2,1)} %gather_fusion, pred[16]{0:T(512)(128)(4,1)S(1)} %compare_and_fusion), kind=kLoop, calls=%fused_computation.27 | loop fusion | flops 1048576 | bytes 4194320 | tf_op jit(solution)/shard_map/jit(_take)/select_n | solution.py:22
  16.3 5.3 %all-to-all-start = ((bf16[16,2,128,256]{3,2,1,0:T(8,128)(2,1)}), bf16[16,2,128,256]{3,2,1,0:T(8,128)(2,1)}, u32[]{:S(2)}, u32[]{:S(2)}) async-start(bf16[16,2,128,256]{3,2,1,0:T(8,128)(2,1)} %broadcast_select_fusion.1), calls=%async_computation | async-start | bytes 4194304 | tf_op jit(solution)/shard_map/all_to_all | solution.py:23
  21.7 26.7 %all-to-all-done = bf16[16,2,128,256]{3,2,1,0:T(8,128)(2,1)} async-done(((bf16[16,2,128,256]{3,2,1,0:T(8,128)(2,1)}), bf16[16,2,128,256]{3,2,1,0:T(8,128)(2,1)}, u32[]{:S(2)}, u32[]{:S(2)}) %all-to-all-start) | async-done | bytes 2097184 | tf_op jit(solution)/shard_map/all_to_all | solution.py:23
  48.3 1.7 copy.32
  50.1 3.5 %copy.33 = bf16[2,2,1024,256]{3,1,2,0:T(2,128)(2,1)} copy(bf16[2,2,1024,256]{3,2,1,0:T(8,128)(2,1)S(1)} %bitcast.96) | data formatting | bytes 4194304 | tf_op jit(solution)/shard_map/all_to_all | solution.py:23
  53.6 20.4 %gather_fusion.2 = bf16[2048,2,256]{2,1,0:T(2,128)(2,1)} fusion(bf16[2,2,1024,256]{3,1,2,0:T(2,128)(2,1)} %copy.33, s32[2048]{0:T(1024)S(1)} %bitcast.88), kind=kCustom, calls=%fused_computation.2 | custom fusion | bytes 4210688 | tf_op jit(solution)/shard_map/vmap()/gather | solution.py:24
  74.0 4.7 %copy.35 = bf16[2,1024,2,256]{1,3,0,2:T(8,128)(2,1)S(1)} copy(bf16[2,1024,2,256]{3,2,1,0:T(2,128)(2,1)} %bitcast.95) | data formatting | bytes 4194304 | tf_op jit(solution)/shard_map/vmap()/gather | solution.py:24
  78.7 83.6 %all-gather.2.cloned.1.call-done = bf16[2,2,1024,1024]{3,2,0,1:T(8,128)(2,1)} async-done(((bf16[2,2,256,1024]{3,2,0,1:T(8,128)(2,1)}), bf16[2,2,1024,1024]{3,2,0,1:T(8,128)(2,1)}) %all-gather.2.cloned.1.call-update) | async-done | bytes 8388624 | tf_op jit(solution)/shard_map/all_gather | solution.py:25
  162.3 3.6 %fusion.2 = f32[2,256,1024]{2,1,0:T(8,128)S(1)} fusion(bf16[2,2,1024,1024]{3,2,0,1:T(8,128)(2,1)} %all-gather.2.cloned.1.call-done, bf16[2,2,1024,256]{2,3,0,1:T(8,128)(2,1)S(1)} %bitcast.98), kind=kOutput, calls=%fused_computation.9 | convolution fusion | flops 1073741824 | bytes 7340032 | tf_op jit(solution)/shard_map/qik,qkj->qij/dot_general | solution.py:10
  165.9 1.0 copy-done.2
  166.9 1.4 fusion.3
  168.3 1.4 fusion.9
  169.8 1.4 fusion.8
  171.2 0.2 fusion.13
  171.4 0.3 pad_maximum_fusion.1
  171.7 51.1 %all_to_all.41 = bf16[4,2,2,256,256]{3,4,1,2,0:T(8,128)(2,1)S(1)} all-to-all(bf16[4,2,2,256,256]{3,4,1,2,0:T(8,128)(2,1)S(1)} %pad_maximum_fusion.1), channel_id=1, replica_groups=mesh['pb'=8,'row'=4] {'row'}, dimensions={0} | all-to-all | bytes 4194304 | tf_op jit(solution)/shard_map/all_to_all | solution.py:29
  222.9 1.3 fusion.1
  224.2 1.3 fusion
  225.6 1.3 subtract_bitcast_fusion
  226.9 1.3 add_bitcast_fusion
  228.3 0.3 pad_maximum_fusion
  228.6 5.2 %copy.40 = f32[2,2,256,1024]{3,0,1,2:T(2,128)} copy(f32[2,2,256,1024]{3,2,0,1:T(8,128)S(1)} %pad_maximum_fusion) | data formatting | bytes 8388608 | tf_op jit(solution)/shard_map/stack | solution.py:14
  233.8 4.8 %all-to-all-start.2 = ((f32[2,2,256,1024]{3,0,1,2:T(2,128)}), f32[2,2,256,1024]{3,0,1,2:T(2,128)}, u32[]{:S(2)}, u32[]{:S(2)}) async-start(f32[2,2,256,1024]{3,0,1,2:T(2,128)} %copy.40), calls=%async_computation.2 | async-start | bytes 8388608 | tf_op jit(solution)/shard_map/all_to_all | solution.py:31
  238.6 48.8 %all-to-all-done.2 = f32[2,2,256,1024]{3,0,1,2:T(2,128)} async-done(((f32[2,2,256,1024]{3,0,1,2:T(2,128)}), f32[2,2,256,1024]{3,0,1,2:T(2,128)}, u32[]{:S(2)}, u32[]{:S(2)}) %all-to-all-start.2) | async-done | bytes 4194336 | tf_op jit(solution)/shard_map/all_to_all | solution.py:31
  287.5 4.6 %copy.41 = f32[2,2,256,1024]{3,2,1,0:T(8,128)S(1)} copy(f32[2,2,256,1024]{3,0,1,2:T(2,128)} %all-to-all-done.2) | data formatting | bytes 8388608 | tf_op jit(solution)/shard_map/all_to_all | solution.py:31
  292.1 2.3 copy.42
  294.4 5.0 %gather_fusion.1 = f32[16,2,32,1024]{3,2,1,0:T(8,128)} fusion(f32[16,2,32,1024]{3,2,1,0:T(8,128)} %bitcast.89, s32[1024]{0:T(1024)S(1)} %pad_clamp_fusion), kind=kCustom, calls=%fused_computation.1 | custom fusion | bytes 8388672 | tf_op jit(solution)/shard_map/jit(_take)/gather | solution.py:32
  299.4 5.3 %broadcast_select_fusion = f32[16,2,32,1024]{3,2,1,0:T(8,128)} fusion(f32[16,2,32,1024]{3,2,1,0:T(8,128)} %gather_fusion.1, pred[16]{0:T(512)(128)(4,1)S(1)} %compare_and_fusion.1), kind=kLoop, calls=%fused_computation.22 | loop fusion | flops 1048576 | bytes 8388624 | tf_op jit(solution)/shard_map/jit(_take)/select_n | solution.py:32
  (20 shorter events, 0.2 us)
Async XLA Ops:
  6.5 4.6 %copy-start = (bf16[16,2,128,256]{3,2,1,0:T(8,128)(2,1)S(1)}, bf16[16,2,128,256]{3,2,1,0:T(8,128)(2,1)}, u32[]{:S(2)}) copy-start(bf16[16,2,128,256]{3,2,1,0:T(8,128)(2,1)} %param.5) | copy-start | bytes 6291460
  6.5 155.7 %all-gather.2.cloned.1.call-start = ((), (), s32[]{:S(2)}) async-start(), calls=%async_computation.3 | async-start | bytes 10485760 | tf_op jit(solution)/shard_map/all_gather | solution.py:25
  9.8 0.7 copy-start.4
  16.3 5.3 %copy-start.3 = (s32[2,1024]{1,0:T(2,128)S(1)}, s32[2,1024]{1,0:T(2,128)}, u32[]{:S(2)}) copy-start(s32[2,1024]{1,0:T(2,128)} %param.7) | copy-start | bytes 24580
  16.3 32.0 %all-to-all-start = ((bf16[16,2,128,256]{3,2,1,0:T(8,128)(2,1)}), bf16[16,2,128,256]{3,2,1,0:T(8,128)(2,1)}, u32[]{:S(2)}, u32[]{:S(2)}) async-start(bf16[16,2,128,256]{3,2,1,0:T(8,128)(2,1)} %broadcast_select_fusion.1), calls=%async_computation | async-start | bytes 4194304 | tf_op jit(solution)/shard_map/all_to_all | solution.py:23
  162.3 4.6 %copy-start.2 = (bf16[2,2,1024,1024]{3,2,0,1:T(8,128)(2,1)S(1)}, bf16[2,2,1024,1024]{3,2,0,1:T(8,128)(2,1)}, u32[]{:S(2)}) copy-start(bf16[2,2,1024,1024]{3,2,0,1:T(8,128)(2,1)} %all-gather.2.cloned.1.call-done) | copy-start | bytes 25165828
  233.8 53.6 %all-to-all-start.2 = ((f32[2,2,256,1024]{3,0,1,2:T(2,128)}), f32[2,2,256,1024]{3,0,1,2:T(2,128)}, u32[]{:S(2)}, u32[]{:S(2)}) async-start(f32[2,2,256,1024]{3,0,1,2:T(2,128)} %copy.40), calls=%async_computation.2 | async-start | bytes 8388608 | tf_op jit(solution)/shard_map/all_to_all | solution.py:31
  299.4 5.3 %copy-start.1 = (bf16[16,2,128,256]{3,2,1,0:T(8,128)(2,1)S(1)}, bf16[16,2,128,256]{3,2,1,0:T(8,128)(2,1)}, u32[]{:S(2)}) copy-start(bf16[16,2,128,256]{3,2,1,0:T(8,128)(2,1)} %param.5) | copy-start | bytes 6291460
Sparse Core Ops, SparseCore 0:
  9.9 152.3 all-gather.1
